TPU v7x, 32 devices: a whole 2x2x4 slice. The times are simulated.
32 devices in a mesh: groups: 1, ctx: 2 (over x), fsdp: 16 (over z, y, core).
Axes of the slice: x: 2, y: 2, z: 4, core: 2. Of those that a mesh axis runs over, the one named last changes fastest.
Arguments:
- tokens: bfloat16 [16, 256, 3072], P(('groups', 'fsdp'), 'ctx'), may hold values from -600 to 600
- trace_index: int32 [16, 256], P(('groups', 'fsdp'), 'ctx'), may hold values from 0 to 1, never falling along the last dimension, each value on 1 to 192 neighbouring positions
- input_norm_scale: bfloat16 [3072], replicated, may hold values from 0.099609375 to 1.8984375
- query_weight: bfloat16 [3072, 2048], P('fsdp'), may hold values from -0.109375 to 0.109375
- key_weight: bfloat16 [3072, 1024], P('fsdp'), may hold values from -0.109375 to 0.109375
- value_weight: bfloat16 [3072, 1024], P('fsdp'), may hold values from -0.109375 to 0.109375
- query_down_weight: bfloat16 [3072, 16], replicated, may hold values from -0.109375 to 0.109375
- query_up_weight: bfloat16 [16, 2048], replicated, may hold values from -1.5 to 1.5
- value_down_weight: bfloat16 [3072, 16], replicated, may hold values from -0.109375 to 0.109375
- value_up_weight: bfloat16 [16, 1024], replicated, may hold values from -1.5 to 1.5
- output_gradient: bfloat16 [16, 256, 2048], P(('groups', 'fsdp'), 'ctx'), may hold values from -24 to 24
Outputs:
- grad_a_query: float32 [3072, 16], P('groups')
- grad_b_query: float32 [16, 2048], P('groups')
- grad_a_value: float32 [3072, 16], P('groups')
- grad_b_value: float32 [16, 1024], P('groups')
Inputs may be any that keep to these rules, and one draw needn't show every extreme that they name: `trace_index`: ids never fall along a sequence; one trace holds at most 192 positions.
All inputs are finite; a program needn't handle non-finite values.
Results may differ from a plain program's by a relative error of at most 0.013.
Values may be sent and summed in bfloat16 or wider, within the bound.
A program may use at most 128 MiB of HBM per device.

v0:
```python
import math
import jax
import jax.numpy as jnp
from jax import lax
from jax.sharding import PartitionSpec as P

HEAD_SIZE = 128
CAP = 50.0
QSCALE = 1.0 / 12.0
ADAPTER_NAME = 0.5
EPS = 1e-06


def shifted(value, axis, by):
    devices = lax.axis_size(axis)
    pairs = [(i, i + by) for i in range(devices) if 0 <= i + by < devices]
    return lax.ppermute(value, axis, pairs)


def normed_rows(values, gain):
    flt = values.astype(jnp.float32)
    meansq = jnp.mean(flt * flt, axis=-1, keepdims=True)
    return (flt * lax.rsqrt(meansq + EPS) * gain.astype(jnp.float32)).astype(jnp.bfloat16)


def add_rows(left, piece):
    return jnp.dot(left, piece, preferred_element_type=jnp.float32)


def attend_head(operands, mask):
    q_head, k_head, v_head, g_head = operands
    s = jnp.einsum("igd,jd->gij", q_head, k_head, preferred_element_type=jnp.float32) * QSCALE
    t = jnp.tanh(s / CAP)
    capped = CAP * t
    expo = jnp.where(mask[None], jnp.exp(capped), jnp.float32(0.0))
    weights = expo / jnp.sum(expo, axis=-1, keepdims=True)
    weights16 = weights.astype(jnp.bfloat16)
    attended = jnp.einsum("gij,jd->igd", weights16, v_head, preferred_element_type=jnp.float32)
    dweight = jnp.einsum("igd,jd->gij", g_head, v_head, preferred_element_type=jnp.float32)
    delta = jnp.sum(g_head.astype(jnp.float32) * attended, axis=-1).T
    dscore = (weights * (dweight - delta[..., None]) * (1.0 - t * t) * QSCALE).astype(jnp.bfloat16)
    query_gradient = jnp.einsum(
        "gij,jd->igd", dscore, k_head, preferred_element_type=jnp.float32
    ).astype(jnp.bfloat16)
    value_gradient = jnp.einsum(
        "gij,igd->jd", weights16, g_head, preferred_element_type=jnp.float32
    )
    return (query_gradient, value_gradient)


def partial_attend(mask):

    def run_head(operands):
        return attend_head(operands, mask)

    return run_head


def on_device(
    tokens,
    trace_index,
    input_norm_scale,
    query_weight,
    key_weight,
    value_weight,
    query_down_weight,
    query_up_weight,
    value_down_weight,
    value_up_weight,
    output_gradient,
):
    window_width = tokens.shape[1]
    feats = tokens.shape[2]
    heads_kv = key_weight.shape[1] // HEAD_SIZE
    heads_q = query_weight.shape[1] // HEAD_SIZE
    head_group = heads_q // heads_kv
    normalized_input = normed_rows(tokens.reshape(window_width, feats), input_norm_scale)
    seg_own = trace_index.reshape(window_width).astype(jnp.bfloat16)
    seg_parts = []

    def add_keyval(piece):
        return add_rows(normalized_input, piece)

    query_frozen = add_rows(
        normalized_input, lax.all_gather(query_weight, "fsdp", axis=0, tiled=True)
    )
    k_base = add_keyval(lax.all_gather(key_weight, "fsdp", axis=0, tiled=True))
    value_frozen = add_keyval(lax.all_gather(value_weight, "fsdp", axis=0, tiled=True))
    query_reduced = jnp.dot(
        normalized_input, query_down_weight, preferred_element_type=jnp.float32
    ).astype(jnp.bfloat16)
    reduced_rows = jnp.dot(
        normalized_input, value_down_weight, preferred_element_type=jnp.float32
    ).astype(jnp.bfloat16)
    query_matrix = (
        query_frozen
        + ADAPTER_NAME * jnp.dot(query_reduced, query_up_weight, preferred_element_type=jnp.float32)
    ).astype(jnp.bfloat16)
    key_rows = k_base.astype(jnp.bfloat16)
    value_rows = (
        value_frozen
        + ADAPTER_NAME * jnp.dot(reduced_rows, value_up_weight, preferred_element_type=jnp.float32)
    ).astype(jnp.bfloat16)
    key_parts = []
    value_parts = []
    for distance in (2, 1):
        key_prev, value_prev, seg_prev = shifted((key_rows, value_rows, seg_own), "ctx", distance)
        key_parts.append(key_prev)
        value_parts.append(value_prev)
        seg_parts.append(seg_prev)
    keys_all = jnp.concatenate(key_parts + [key_rows], 0)
    values_all = jnp.concatenate(value_parts + [value_rows], 0)
    seg_keys = jnp.concatenate(seg_parts + [seg_own], 0)
    pos_q = jnp.arange(window_width, dtype=jnp.int32)[:, None]
    pos_k = jnp.arange(3 * window_width, dtype=jnp.int32)[None, :]
    position = lax.axis_index("ctx")
    mask = (
        (pos_k > pos_q)
        & (pos_k <= pos_q + 2 * window_width)
        & (seg_keys[None, :] == seg_own[:, None])
    )
    mask = mask & (
        (pos_k >= 2 * window_width) | (pos_k >= window_width) & (position >= 1) | (position >= 2)
    )
    q_heads = jnp.moveaxis(
        query_matrix.reshape(window_width, heads_kv, head_group, HEAD_SIZE), 1, 0
    )
    g_heads = jnp.moveaxis(
        output_gradient.reshape(window_width, heads_kv, head_group, HEAD_SIZE), 1, 0
    )
    k_heads = jnp.moveaxis(keys_all.reshape(3 * window_width, heads_kv, HEAD_SIZE), 1, 0)
    v_heads = jnp.moveaxis(values_all.reshape(3 * window_width, heads_kv, HEAD_SIZE), 1, 0)
    dquery_heads, dvalue_heads = lax.map(partial_attend(mask), (q_heads, k_heads, v_heads, g_heads))
    query_gradient = jnp.moveaxis(dquery_heads, 0, 1).reshape(window_width, heads_q * HEAD_SIZE)
    dvalue_triple = jnp.moveaxis(dvalue_heads, 0, 1).reshape(3 * window_width, heads_kv * HEAD_SIZE)
    value_gradient = dvalue_triple[2 * window_width :]
    for distance in (1, 2):
        begin = (2 - distance) * window_width
        value_gradient = value_gradient + shifted(
            dvalue_triple[begin : begin + window_width], "ctx", -distance
        )
    query_backward = jnp.dot(
        query_gradient, query_up_weight.T, preferred_element_type=jnp.float32
    ).astype(jnp.bfloat16)
    value_backward = jnp.dot(
        value_gradient, value_up_weight.astype(jnp.float32).T, precision=lax.Precision.HIGHEST
    )
    part_aq = jnp.dot(normalized_input.T, query_backward, preferred_element_type=jnp.float32)
    part_bq = jnp.dot(query_reduced.T, query_gradient, preferred_element_type=jnp.float32)
    part_av = jnp.dot(
        normalized_input.astype(jnp.float32).T, value_backward, precision=lax.Precision.HIGHEST
    )
    part_bv = jnp.dot(
        reduced_rows.astype(jnp.float32).T, value_gradient, precision=lax.Precision.HIGHEST
    )
    sum_aq, sum_bq, sum_av, sum_bv = lax.psum((part_aq, part_bq, part_av, part_bv), ("ctx", "fsdp"))
    token_total = lax.axis_size("ctx") * lax.axis_size("fsdp") * window_width
    coefficient = ADAPTER_NAME / math.sqrt(token_total)
    return (sum_aq * coefficient, sum_bq * coefficient, sum_av * coefficient, sum_bv * coefficient)


def solution(mesh):
    return jax.shard_map(
        on_device,
        mesh=mesh,
        in_specs=(
            P(("groups", "fsdp"), "ctx", None),
            P(("groups", "fsdp"), "ctx"),
            P(),
            P("fsdp", None),
            P("fsdp", None),
            P("fsdp", None),
            P(),
            P(),
            P(),
            P(),
            P(("groups", "fsdp"), "ctx", None),
        ),
        out_specs=(P("groups", None), P("groups", None), P("groups", None), P("groups", None)),
        check_vma=False,
    )
```

profile of v0, /device:TPU:0, one launch (start us, length us, event | category | flops | bytes accessed | tf_op | source)
XLA Modules:
  0.0 444.9 jit_solution(15233795654485202083)
XLA Ops:
  7.3 0.7 all-gather.8.cloned.1.call-update
  8.0 0.7 all-gather.4.cloned.1.call-update
  8.8 0.7 all-gather.6.cloned.1.call-update
  9.5 0.7 collective-permute-start.2
  10.2 0.5 iota_add_fusion
  11.0 0.4 convolution_convert_fusion.2
  11.3 1.0 convolution_convert_fusion.3
  12.4 62.1 %all-gather.8.cloned.1.call-done = bf16[3072,1024]{1,0:T(8,128)(2,1)} async-done(((bf16[192,1024]{1,0:T(8,128)(2,1)}), bf16[3072,1024]{1,0:T(8,128)(2,1)}) %all-gather.8.cloned.1.call-update) | async-done | bytes 6291472 | tf_op jit(solution)/shard_map/all_gather | solution.py:88
  74.5 3.8 fusion.71
  78.6 0.8 collective-permute-start.4
  79.4 3.4 collective-permute-start.5
  82.8 54.1 %all-gather.4.cloned.1.call-done = bf16[3072,1024]{1,0:T(8,128)(2,1)} async-done(((bf16[192,1024]{1,0:T(8,128)(2,1)}), bf16[3072,1024]{1,0:T(8,128)(2,1)}) %all-gather.4.cloned.1.call-update) | async-done | bytes 6291472 | tf_op jit(solution)/shard_map/all_gather | solution.py:87
  136.9 3.8 convolution_convert_fusion
  140.7 0.7 collective-permute-start
  141.4 4.1 collective-permute-start.1
  145.5 0.5 fusion.65
  146.0 1.3 collective-permute-start.3
  147.6 3.2 collective-permute-done.3
  151.0 2.0 bitcast_bitcast_fusion.1
  153.0 85.4 %all-gather.6.cloned.1.call-done = bf16[3072,2048]{1,0:T(8,128)(2,1)} async-done(((bf16[192,2048]{1,0:T(8,128)(2,1)}), bf16[3072,2048]{1,0:T(8,128)(2,1)}) %all-gather.6.cloned.1.call-update) | async-done | bytes 12582928 | tf_op jit(solution)/shard_map/all_gather | solution.py:85
  238.3 6.4 %fusion.74 = f32[128,2048]{1,0:T(8,128)S(1)} fusion(bf16[3072,2048]{1,0:T(8,128)(2,1)} %all-gather.6.cloned.1.call-done, bf16[1,128,3072]{2,1,0:T(8,128)(2,1)S(1)} %copy-done.1, f32[3072]{0:T(1024)S(1)} %convert_element_type.72, f32[128]{0:T(128)} %copy-done.14), kind=kOutput, calls=%fused_computation.95 | convolution fusion | flops 1612185600 | bytes 14430720 | tf_op jit(solution)/shard_map/dot_general | solution.py:27
  245.5 0.9 copy.40
  246.4 38.3 %while.15 = (s32[]{:T(128)}, bf16[8,128,2,128]{1,3,2,0:T(8,128)(2,1)}, f32[8,384,128]{1,2,0:T(8,128)}, bf16[8,384,128]{2,1,0:T(8,128)(2,1)}, bf16[8,128,2,128]{3...) while((s32[]{:T(128)}, ...), condition=%wide.region_4.5_spmd.clone, body=%wide.region_1.4_spmd.clone.sunk | while | flops 128122368 | bytes 3156989 | solution.py:133
  246.6 1.2 fusion.122
  247.9 0.9 fusion.126
  248.9 0.4 fusion.124
  249.3 1.9 fusion.125
  251.4 1.2 fusion.122
  252.7 0.9 fusion.126
  253.7 0.4 fusion.124
  254.1 1.9 fusion.125
  256.2 1.2 fusion.122
  257.5 0.9 fusion.126
  258.5 0.4 fusion.124
  258.9 1.9 fusion.125
  261.0 1.2 fusion.122
  262.3 0.9 fusion.126
  263.7 1.9 fusion.125
  265.8 1.2 fusion.122
  267.1 0.9 fusion.126
  268.5 1.9 fusion.125
  270.6 1.2 fusion.122
  271.9 0.9 fusion.126
  273.3 1.9 fusion.125
  275.3 1.2 fusion.122
  276.6 0.9 fusion.126
  278.0 1.9 fusion.125
  280.1 1.2 fusion.122
  281.4 0.9 fusion.126
  282.8 1.9 fusion.125
  284.7 1.5 fusion.77
  286.3 1.3 collective-permute-start.6
  287.6 1.5 collective-permute-start.7
  289.0 0.9 fusion.78
  289.9 2.3 fusion.62
  292.2 10.1 %collective-permute-done.6 = f32[128,1024]{0,1:T(8,128)S(1)} collective-permute-done((f32[128,1024]{0,1:T(8,128)S(1)}, f32[128,1024]{0,1:T(8,128)S(1)}, u32[]{:S(2)}, u32[]{:S(2)}) %collective-permute-start.6) | collective-permute-done | bytes 524320 | tf_op jit(solution)/shard_map/ppermute | solution.py:17
  302.3 1.1 fusion.63
  303.4 0.6 fusion.79
  304.0 1.0 fusion.80
  305.0 1.3 fusion.67
  306.2 127.3 %all-reduce.3.cloned.1.call-done = (f32[3072,16]{0,1:T(8,128)}, f32[16,2048]{1,0:T(8,128)}, f32[3072,16]{0,1:T(8,128)}, f32[16,1024]{1,0:T(8,128)}) async-done(((f32[3072,16]{0,1:T(8,128)}, f32[16,2048]{1,0:T(8,128)}, f32[3072,16]{0,1:T(8,128)}, f32[16,1024]{1,0:T(8,128)}), (f32[3072,16]{0,1:T(8,128)}, f32[16,2048]{1,0:T(8,128)}, f32[3072,16]{0,1:T(8,128)}, ...) | async-done | bytes 589840 | tf_op jit(solution)/shard_map/psum | solution.py:156
  433.5 1.6 broadcast_multiply_fusion.2
  435.1 1.5 broadcast_multiply_fusion.3
  436.5 1.8 broadcast_multiply_fusion
  (98 shorter events, 6.9 us)
Async XLA Ops:
  7.2 3.8 copy-start
  7.2 2.3 copy-start.18
  7.2 3.0 copy-start.16
  7.2 3.5 copy-start.1
  7.2 67.2 %all-gather.8.cloned.1.call-start = ((), (), s32[]{:S(2)}) async-start(), calls=%async_computation.2 | async-start | bytes 6684672 | tf_op jit(solution)/shard_map/all_gather | solution.py:88
  7.9 128.9 %all-gather.4.cloned.1.call-start = ((), (), s32[]{:S(2)}) async-start(), calls=%async_computation | async-start | bytes 6684672 | tf_op jit(solution)/shard_map/all_gather | solution.py:87
  8.7 2.7 copy-start.17
  8.7 229.6 %all-gather.6.cloned.1.call-start = ((), (), s32[]{:S(2)}) async-start(), calls=%async_computation.1 | async-start | bytes 13369344 | tf_op jit(solution)/shard_map/all_gather | solution.py:85
  9.4 424.1 %all-reduce.3.cloned.1.call-start = ((), (), s32[]{:S(2)}) async-start(), calls=%async_computation.3 | async-start | bytes 1179648 | tf_op jit(solution)/shard_map/psum | solution.py:156
  9.5 141.3 %copy-start.6 = (bf16[128]{0:T(256)(128)(2,1)}, bf16[128]{0:T(256)(128)(2,1)S(1)}, u32[]{:S(2)}) copy-start(bf16[128]{0:T(256)(128)(2,1)S(1)} %convert_bitcast_fusion) | copy-start | bytes 772
  9.5 136.5 %collective-permute-start.2 = (bf16[128]{0:T(256)(128)(2,1)S(1)}, bf16[128]{0:T(256)(128)(2,1)S(1)}, u32[]{:S(2)}, u32[]{:S(2)}) collective-permute-start(bf16[128]{0:T(256)(128)(2,1)S(1)} %convert_bitcast_fusion), channel_id=1, source_target_pairs={} | collective-permute-start | bytes 776 | tf_op jit(solution)/shard_map/ppermute | solution.py:17
  11.0 125.9 %copy-start.14 = (f32[128]{0:T(128)}, f32[128]{0:T(128)S(1)}, u32[]{:S(2)}) copy-start(f32[128]{0:T(128)S(1)} %add_rsqrt_fusion) | copy-start | bytes 1540
  11.3 66.9 %copy-start.8 = (bf16[128,16]{0,1:T(8,128)(2,1)}, bf16[128,16]{0,1:T(8,128)(2,1)S(1)}, u32[]{:S(2)}) copy-start(bf16[128,16]{0,1:T(8,128)(2,1)S(1)} %convolution_convert_fusion.2) | copy-start | bytes 12292
  12.4 65.9 %copy-start.4 = (bf16[16,1024]{1,0:T(8,128)(2,1)S(1)}, bf16[16,1024]{1,0:T(8,128)(2,1)}, u32[]{:S(2)}) copy-start(bf16[16,1024]{1,0:T(8,128)(2,1)} %param.22) | copy-start | bytes 98308
  78.5 68.8 %copy-start.3 = (bf16[1,128,2048]{2,1,0:T(8,128)(2,1)S(1)}, bf16[1,128,2048]{2,1,0:T(8,128)(2,1)}, u32[]{:S(2)}) copy-start(bf16[1,128,2048]{2,1,0:T(8,128)(2,1)} %param.23) | copy-start | bytes 1572868
  78.6 72.2 %collective-permute-start.4 = (bf16[128,1024]{1,0:T(8,128)(2,1)S(1)}, bf16[128,1024]{1,0:T(8,128)(2,1)S(1)}, u32[]{:S(2)}, u32[]{:S(2)}) collective-permute-start(bf16[128,1024]{1,0:T(8,128)(2,1)S(1)} %fusion.61), channel_id=1, source_target_pairs={} | collective-permute-start | bytes 786440 | tf_op jit(solution)/shard_map/ppermute | solution.py:17
  79.4 71.4 %collective-permute-start.5 = (bf16[128,1024]{1,0:T(8,128)(2,1)S(1)}, bf16[128,1024]{1,0:T(8,128)(2,1)S(1)}, u32[]{:S(2)}, u32[]{:S(2)}) collective-permute-start(bf16[128,1024]{1,0:T(8,128)(2,1)S(1)} %fusion.61), channel_id=1, source_target_pairs={{0,16},{1,17},{2,18},{3,19},{4,20},{5,21},{6,22},{7,23},{8,24},{9,... | collective-permute-start | bytes 786440 | tf_op jit(solution)/shard_map/ppermute | solution.py:17
  140.7 10.2 %collective-permute-start = (bf16[128,1024]{1,0:T(8,128)(2,1)S(1)}, bf16[128,1024]{1,0:T(8,128)(2,1)S(1)}, u32[]{:S(2)}, u32[]{:S(2)}) collective-permute-start(bf16[128,1024]{1,0:T(8,128)(2,1)S(1)} %convolution_convert_fusion), channel_id=1, source_target_pairs={} | collective-permute-start | bytes 786440 | tf_op jit(solution)/shard_map/ppermute | solution.py:17
  141.4 9.6 %collective-permute-start.1 = (bf16[128,1024]{1,0:T(8,128)(2,1)S(1)}, bf16[128,1024]{1,0:T(8,128)(2,1)}, u32[]{:S(2)}, u32[]{:S(2)}) collective-permute-start(bf16[128,1024]{1,0:T(8,128)(2,1)S(1)} %convolution_convert_fusion), channel_id=1, source_target_pairs={{0,16},{1,17},{2,18},{3,19},{4,20},{5,21},{6,22},{7,23},{8,24},{9,... | collective-permute-start | bytes 786440 | tf_op jit(solution)/shard_map/ppermute | solution.py:17
  146.0 4.8 %collective-permute-start.3 = (bf16[128]{0:T(256)(128)(2,1)S(1)}, bf16[128]{0:T(256)(128)(2,1)S(1)}, u32[]{:S(2)}, u32[]{:S(2)}) collective-permute-start(bf16[128]{0:T(256)(128)(2,1)S(1)} %convert_bitcast_fusion), channel_id=1, source_target_pairs={{0,16},{1,17},{2,18},{3,19},{4,20},{5,21},{6,22},{7,23},{8,24},{9,... | collective-permute-start | bytes 776 | tf_op jit(solution)/shard_map/ppermute | solution.py:17
  153.0 91.8 %copy-start.5 = (bf16[16,2048]{1,0:T(8,128)(2,1)S(1)}, bf16[16,2048]{1,0:T(8,128)(2,1)}, u32[]{:S(2)}) copy-start(bf16[16,2048]{1,0:T(8,128)(2,1)} %param.20) | copy-start | bytes 196612
  153.0 91.8 %copy-start.10 = (bf16[128,16]{0,1:T(8,128)(2,1)S(1)}, bf16[128,16]{0,1:T(8,128)(2,1)}, u32[]{:S(2)}) copy-start(bf16[128,16]{0,1:T(8,128)(2,1)} %convolution_convert_fusion.3) | copy-start | bytes 12292
  244.8 1.7 copy-start.7
  244.8 1.6 copy-start.12
  244.8 1.6 copy-start.13
  284.7 4.3 copy-start.2
  284.7 4.3 copy-start.11
  284.7 5.2 %copy-start.15 = (f32[128]{0:T(128)S(1)}, f32[128]{0:T(128)}, u32[]{:S(2)}) copy-start(f32[128]{0:T(128)} %copy-done.14) | copy-start | bytes 1540
  286.3 16.0 %collective-permute-start.6 = (f32[128,1024]{0,1:T(8,128)S(1)}, f32[128,1024]{0,1:T(8,128)S(1)}, u32[]{:S(2)}, u32[]{:S(2)}) collective-permute-start(f32[128,1024]{0,1:T(8,128)S(1)} %bitcast.193), channel_id=1, source_target_pairs={{16,0},{17,1},{18,2},{19,3},{20,4},{21,5},{22,6},{23,7},{24,8},{25... | collective-permute-start | bytes 1572872 | tf_op jit(solution)/shard_map/ppermute | solution.py:17
  287.6 14.7 %collective-permute-start.7 = (f32[128,1024]{0,1:T(8,128)S(1)}, f32[128,1024]{0,1:T(8,128)}, u32[]{:S(2)}, u32[]{:S(2)}) collective-permute-start(f32[128,1024]{0,1:T(8,128)S(1)} %bitcast.192), channel_id=1, source_target_pairs={} | collective-permute-start | bytes 1572872 | tf_op jit(solution)/shard_map/ppermute | solution.py:17
  292.2 11.8 %copy-start.9 = (bf16[128,16]{0,1:T(8,128)(2,1)S(1)}, bf16[128,16]{0,1:T(8,128)(2,1)}, u32[]{:S(2)}) copy-start(bf16[128,16]{0,1:T(8,128)(2,1)} %copy-done.8) | copy-start | bytes 12292
Sparse Core Ops, SparseCore 0:
  10.3 64.1 all-gather.7
  76.7 60.0 all-gather.3
  139.2 99.1 all-gather.5
  306.4 127.0 all-reduce.2
where the time goes:
time: 446 us; the launch traced here: 445 us
  waiting for transfers between devices  344 us (77%)
  matrix products  57 us (13%)
  between operations  14.1 us (3%)
  starting transfers between devices  13.8 us (3%)
  other arithmetic  11.5 us (3%)
    psum x1, waiting for transfers between devices, on_device(): lax.psum((part_aq, part_bq, part_av, part_bv), ('ctx', 'fsdp'))  127 us
    all_gather x1, waiting for transfers between devices, on_device(): lax.all_gather(query_weight, 'fsdp', axis=0, tiled=True)  85.4 us
    all_gather x1, waiting for transfers between devices, on_device(): lax.all_gather(value_weight, 'fsdp', axis=0, tiled=True)  62.1 us
    all_gather x1, waiting for transfers between devices, on_device(): k_base = add_keyval(lax.all_gather(key_weight, 'fsdp', axis=0, tiled=True))  54.1 us
    dot_general x8, matrix products, attend_head(): jnp.einsum('gij,jd->igd', dscore, k_head, preferred_element_type=jnp.floa...  15.3 us
    dot_general x3, matrix products, add_rows(): return jnp.dot(left, piece, preferred_element_type=jnp.float32)  14.1 us
    ppermute x8, starting transfers between devices, shifted(): return lax.ppermute(value, axis, pairs)  13.6 us
    ppermute x8, waiting for transfers between devices, shifted(): return lax.ppermute(value, axis, pairs)  13.2 us
  transfers between devices with their start and end apart: 12, of which 6 were waited for; matrix products, arithmetic and copies ran while one was open for 4% of the time, Pallas kernels for 0%

commit v1 on v0

--- a/solution.py
+++ b/solution.py
@@ -9,6 +9,19 @@
 QSCALE = 1.0 / 12.0
 ADAPTER_NAME = 0.5
 EPS = 1e-06
+
+
+def ring_gather(array, axis, dim):
+    ways = lax.axis_size(axis)
+    up = [(d, (d + 1) % ways) for d in range(ways)]
+    down = [(d, (d - 1) % ways) for d in range(ways)]
+    earlier, later = ([array], [array])
+    for _ in range(ways // 2):
+        earlier.append(lax.ppermute(earlier[-1], axis, up))
+    for _ in range((ways - 1) // 2):
+        later.append(lax.ppermute(later[-1], axis, down))
+    line = jnp.concatenate([*earlier[::-1], *later[1:]], axis=dim)
+    return jnp.roll(line, (lax.axis_index(axis) - ways // 2) * array.shape[dim], axis=dim)
 
 
 def shifted(value, axis, by):
@@ -85,7 +98,7 @@
         normalized_input, lax.all_gather(query_weight, "fsdp", axis=0, tiled=True)
     )
     k_base = add_keyval(lax.all_gather(key_weight, "fsdp", axis=0, tiled=True))
-    value_frozen = add_keyval(lax.all_gather(value_weight, "fsdp", axis=0, tiled=True))
+    value_frozen = add_keyval(ring_gather(value_weight, "fsdp", 0))
     query_reduced = jnp.dot(
         normalized_input, query_down_weight, preferred_element_type=jnp.float32
     ).astype(jnp.bfloat16)

time: 446 us -> 415 us (0.930)
  waiting for transfers between devices: 344 us -> 259 us
  starting transfers between devices: 13.8 us -> 43.9 us
  local copies, waits for them, and re-layouts: 4.18 us -> 21.1 us
    all_gather x1 -> x0, waiting for transfers between devices: 62.1 us -> none  [on_device(): lax.all_gather(value_weight, 'fsdp', axis=0, tiled=True)]
    ppermute x0 -> x15, waiting for transfers between devices: none -> 59.5 us  [the longest x8 49 us: ring_gather(): earlier.append(lax.ppermute(earlier[-1], axis, up))]
    all_gather x1, waiting for transfers between devices: 54.1 us -> 0.02 us  [on_device(): k_base = add_keyval(lax.all_gather(key_weight, 'fsdp', axis=0, tiled=True))]
    ppermute x0 -> x15, starting transfers between devices: none -> 32.1 us  [the longest x7 31.5 us: ring_gather(): later.append(lax.ppermute(later[-1], axis, down))]
    all_gather x1, waiting for transfers between devices: 85.4 us -> 59.9 us  [on_device(): lax.all_gather(query_weight, 'fsdp', axis=0, tiled=True)]
    unnamed x39 -> x78, local copies, waits for them, and re-layouts: 0.35 us -> 17.3 us
  transfers between devices with their start and end apart: 12 -> 26, of which waited for: 6 -> 12; matrix products, arithmetic and copies ran while one was open for 4% -> 9% of each run, Pallas kernels for 0% -> 0%
where the time goes in v1:
time: 415 us; the launch traced here: 413 us
  waiting for transfers between devices  259 us (62%)
  matrix products  61.3 us (15%)
  starting transfers between devices  43.9 us (11%)
  local copies, waits for them, and re-layouts  21.1 us (5%)
  between operations  14.4 us (3%)
  other arithmetic  13 us (3%)
    psum x1, waiting for transfers between devices, on_device(): lax.psum((part_aq, part_bq, part_av, part_bv), ('ctx', 'fsdp'))  127 us
    all_gather x1, waiting for transfers between devices, on_device(): lax.all_gather(query_weight, 'fsdp', axis=0, tiled=True)  59.9 us
    ppermute x8, waiting for transfers between devices, ring_gather(): earlier.append(lax.ppermute(earlier[-1], axis, up))  49 us
    ppermute x7, starting transfers between devices, ring_gather(): later.append(lax.ppermute(later[-1], axis, down))  31.5 us
    unnamed x78, local copies, waits for them, and re-layouts  17.3 us
    dot_general x8, matrix products, attend_head(): jnp.einsum('gij,jd->igd', dscore, k_head, preferred_element_type=jnp.floa...  15.3 us
    dot_general x3, matrix products, add_rows(): return jnp.dot(left, piece, preferred_element_type=jnp.float32)  12.3 us
    ppermute x8, starting transfers between devices, shifted(): return lax.ppermute(value, axis, pairs)  11.6 us
  transfers between devices with their start and end apart: 26, of which 12 were waited for; matrix products, arithmetic and copies ran while one was open for 9% of the time, Pallas kernels for 0%

profile of v1, /device:TPU:0, one launch (start us, length us, event | category | flops | bytes accessed | tf_op | source)
XLA Modules:
  0.0 412.6 jit_solution(3464661252372470598)
XLA Ops:
  9.3 10.7 %collective-permute-done.4 = bf16[192,1024]{1,0:T(8,128)(2,1)S(1)} collective-permute-done((bf16[192,1024]{1,0:T(8,128)(2,1)}, bf16[192,1024]{1,0:T(8,128)(2,1)S(1)}, u32[]{:S(2)}, u32[]{:S(2)}) %collective-permute-start.4) | collective-permute-done | bytes 393248 | tf_op jit(solution)/shard_map/ppermute | solution.py:20
  19.9 4.4 %collective-permute-start.12 = (bf16[192,1024]{1,0:T(8,128)(2,1)}, bf16[192,1024]{1,0:T(8,128)(2,1)S(1)}, u32[]{:S(2)}, u32[]{:S(2)}) collective-permute-start(bf16[192,1024]{1,0:T(8,128)(2,1)} %param.18), channel_id=1, source_target_pairs={{0,15},{1,0},{2,1},{3,2},{4,3},{5,4},{6,5},{7,6},{8,7},{9,8},{10,9... | collective-permute-start | bytes 1179656 | tf_op jit(solution)/shard_map/ppermute | solution.py:22
  24.4 11.6 %collective-permute-done.5 = bf16[192,1024]{1,0:T(8,128)(2,1)S(1)} collective-permute-done((bf16[192,1024]{1,0:T(8,128)(2,1)S(1)}, bf16[192,1024]{1,0:T(8,128)(2,1)S(1)}, u32[]{:S(2)}, u32[]{:S(2)}) %collective-permute-start.5) | collective-permute-done | bytes 393248 | tf_op jit(solution)/shard_map/ppermute | solution.py:20
  35.9 4.4 %collective-permute-start.13 = (bf16[192,1024]{1,0:T(8,128)(2,1)S(1)}, bf16[192,1024]{1,0:T(8,128)(2,1)S(1)}, u32[]{:S(2)}, u32[]{:S(2)}) collective-permute-start(bf16[192,1024]{1,0:T(8,128)(2,1)S(1)} %collective-permute-done.12), channel_id=1, source_target_pairs={{0,15},{1,0},{2,1},{3,2},{4,3},{5,4},{6,5},{7,6},{8,7},{9,8},{10,9... | collective-permute-start | bytes 1179656 | tf_op jit(solution)/shard_map/ppermute | solution.py:22
  40.4 7.0 %collective-permute-done.6 = bf16[192,1024]{1,0:T(8,128)(2,1)S(1)} collective-permute-done((bf16[192,1024]{1,0:T(8,128)(2,1)S(1)}, bf16[192,1024]{1,0:T(8,128)(2,1)S(1)}, u32[]{:S(2)}, u32[]{:S(2)}) %collective-permute-start.6) | collective-permute-done | bytes 393248 | tf_op jit(solution)/shard_map/ppermute | solution.py:20
  47.4 4.4 %collective-permute-start.14 = (bf16[192,1024]{1,0:T(8,128)(2,1)S(1)}, bf16[192,1024]{1,0:T(8,128)(2,1)S(1)}, u32[]{:S(2)}, u32[]{:S(2)}) collective-permute-start(bf16[192,1024]{1,0:T(8,128)(2,1)S(1)} %collective-permute-done.13), channel_id=1, source_target_pairs={{0,15},{1,0},{2,1},{3,2},{4,3},{5,4},{6,5},{7,6},{8,7},{9,8},{10,9... | collective-permute-start | bytes 1179656 | tf_op jit(solution)/shard_map/ppermute | solution.py:22
  51.9 13.9 %collective-permute-done.7 = bf16[192,1024]{1,0:T(8,128)(2,1)S(1)} collective-permute-done((bf16[192,1024]{1,0:T(8,128)(2,1)S(1)}, bf16[192,1024]{1,0:T(8,128)(2,1)S(1)}, u32[]{:S(2)}, u32[]{:S(2)}) %collective-permute-start.7) | collective-permute-done | bytes 393248 | tf_op jit(solution)/shard_map/ppermute | solution.py:20
  65.8 4.5 %collective-permute-start.15 = (bf16[192,1024]{1,0:T(8,128)(2,1)S(1)}, bf16[192,1024]{1,0:T(8,128)(2,1)S(1)}, u32[]{:S(2)}, u32[]{:S(2)}) collective-permute-start(bf16[192,1024]{1,0:T(8,128)(2,1)S(1)} %collective-permute-done.14), channel_id=1, source_target_pairs={{0,15},{1,0},{2,1},{3,2},{4,3},{5,4},{6,5},{7,6},{8,7},{9,8},{10,9... | collective-permute-start | bytes 1179656 | tf_op jit(solution)/shard_map/ppermute | solution.py:22
  70.3 5.8 %collective-permute-done.8 = bf16[192,1024]{1,0:T(8,128)(2,1)S(1)} collective-permute-done((bf16[192,1024]{1,0:T(8,128)(2,1)S(1)}, bf16[192,1024]{1,0:T(8,128)(2,1)S(1)}, u32[]{:S(2)}, u32[]{:S(2)}) %collective-permute-start.8) | collective-permute-done | bytes 393248 | tf_op jit(solution)/shard_map/ppermute | solution.py:20
  77.5 3.0 collective-permute-start.3
  81.2 1.4 fusion.59
  82.6 4.2 %collective-permute-start.16 = (bf16[192,1024]{1,0:T(8,128)(2,1)S(1)}, bf16[192,1024]{1,0:T(8,128)(2,1)}, u32[]{:S(2)}, u32[]{:S(2)}) collective-permute-start(bf16[192,1024]{1,0:T(8,128)(2,1)S(1)} %collective-permute-done.15), channel_id=1, source_target_pairs={{0,15},{1,0},{2,1},{3,2},{4,3},{5,4},{6,5},{7,6},{8,7},{9,8},{10,9... | collective-permute-start | bytes 1179656 | tf_op jit(solution)/shard_map/ppermute | solution.py:22
  86.9 1.6 convolution_convert_fusion.2
  88.5 5.9 %collective-permute-done.16 = bf16[192,1024]{1,0:T(8,128)(2,1)} collective-permute-done((bf16[192,1024]{1,0:T(8,128)(2,1)S(1)}, bf16[192,1024]{1,0:T(8,128)(2,1)}, u32[]{:S(2)}, u32[]{:S(2)}) %collective-permute-start.16) | collective-permute-done | bytes 393248 | tf_op jit(solution)/shard_map/ppermute | solution.py:22
  94.4 4.8 %collective-permute-start.17 = (bf16[192,1024]{1,0:T(8,128)(2,1)}, bf16[192,1024]{1,0:T(8,128)(2,1)}, u32[]{:S(2)}, u32[]{:S(2)}) collective-permute-start(bf16[192,1024]{1,0:T(8,128)(2,1)} %collective-permute-done.16), channel_id=1, source_target_pairs={{0,15},{1,0},{2,1},{3,2},{4,3},{5,4},{6,5},{7,6},{8,7},{9,8},{10,9... | collective-permute-start | bytes 1179656 | tf_op jit(solution)/shard_map/ppermute | solution.py:22
  100.9 1.7 convolution_convert_fusion.3
  102.5 2.3 collective-permute-done.17
  104.8 4.7 %collective-permute-start.18 = (bf16[192,1024]{1,0:T(8,128)(2,1)}, bf16[192,1024]{1,0:T(8,128)(2,1)S(1)}, u32[]{:S(2)}, u32[]{:S(2)}) collective-permute-start(bf16[192,1024]{1,0:T(8,128)(2,1)} %collective-permute-done.17), channel_id=1, source_target_pairs={{0,15},{1,0},{2,1},{3,2},{4,3},{5,4},{6,5},{7,6},{8,7},{9,8},{10,9... | collective-permute-start | bytes 1179656 | tf_op jit(solution)/shard_map/ppermute | solution.py:22
  109.5 1.1 constant_dynamic-update-slice_fusion.31
  110.6 1.1 constant_dynamic-update-slice_fusion.30
  111.7 1.0 constant_dynamic-update-slice_fusion.29
  112.7 1.0 constant_dynamic-update-slice_fusion.28
  113.7 1.0 constant_dynamic-update-slice_fusion.27
  114.8 1.0 constant_dynamic-update-slice_fusion.26
  115.9 1.0 constant_dynamic-update-slice_fusion.23
  121.1 2.3 collective-permute-done.18
  128.0 2.0 fusion.65
  130.8 2.7 collective-permute-start.20
  133.4 3.8 convolution_convert_fusion
  138.0 2.0 collective-permute-start.1
  140.6 1.3 copy.25
  142.1 1.1 collective-permute-done.1
  143.2 2.0 bitcast_bitcast_fusion.1
  145.2 59.9 %all-gather.5.cloned.1.call-done = bf16[3072,2048]{1,0:T(8,128)(2,1)} async-done(((bf16[192,2048]{1,0:T(8,128)(2,1)}), bf16[3072,2048]{1,0:T(8,128)(2,1)}) %all-gather.5.cloned.1.call-update) | async-done | bytes 12582928 | tf_op jit(solution)/shard_map/all_gather | solution.py:98
  205.1 6.4 %fusion.80 = f32[128,2048]{1,0:T(8,128)S(1)} fusion(bf16[3072,2048]{1,0:T(8,128)(2,1)} %all-gather.5.cloned.1.call-done, bf16[1,128,3072]{2,1,0:T(8,128)(2,1)S(1)} %copy-done.1, f32[3072]{0:T(1024)S(1)} %convert_element_type.72, f32[128]{0:T(128)S(1)} %add_rsqrt_fusion), kind=kOutput, calls=%fused_computation.129 | convolution fusion | flops 1612185600 | bytes 14430720 | tf_op jit(solution)/shard_map/dot_general | solution.py:40
  211.5 1.2 fusion.58
  214.0 38.3 %while.15 = (s32[]{:T(128)}, bf16[8,128,2,128]{1,3,2,0:T(8,128)(2,1)}, f32[8,384,128]{1,2,0:T(8,128)}, bf16[8,384,128]{2,1,0:T(8,128)(2,1)}, bf16[8,128,2,128]{3...) while((s32[]{:T(128)}, ...), condition=%wide.region_4.5_spmd.clone, body=%wide.region_1.4_spmd.clone.sunk | while | flops 128122368 | bytes 3156989 | solution.py:146
  214.2 1.2 fusion.127
  216.9 1.9 fusion.130
  219.0 1.2 fusion.127
  221.7 1.9 fusion.130
  223.8 1.2 fusion.127
  226.5 1.9 fusion.130
  228.6 1.2 fusion.127
  231.2 1.9 fusion.130
  233.3 1.2 fusion.127
  236.0 1.9 fusion.130
  238.1 1.2 fusion.127
  240.8 1.9 fusion.130
  242.9 1.2 fusion.127
  245.6 1.9 fusion.130
  247.7 1.2 fusion.127
  250.4 1.9 fusion.130
  252.3 1.5 fusion.83
  253.8 1.3 collective-permute-start.21
  255.8 2.0 fusion.84
  257.7 2.5 fusion.68
  260.2 9.5 %collective-permute-done.21 = f32[128,1024]{0,1:T(8,128)S(1)} collective-permute-done((f32[128,1024]{0,1:T(8,128)S(1)}, f32[128,1024]{0,1:T(8,128)S(1)}, u32[]{:S(2)}, u32[]{:S(2)}) %collective-permute-start.21) | collective-permute-done | bytes 524320 | tf_op jit(solution)/shard_map/ppermute | solution.py:30
  270.4 1.7 fusion.86
  272.1 1.9 fusion.74
  274.0 127.2 %all-reduce.3.cloned.1.call-done = (f32[3072,16]{0,1:T(8,128)}, f32[16,2048]{1,0:T(8,128)}, f32[3072,16]{0,1:T(8,128)}, f32[16,1024]{1,0:T(8,128)}) async-done(((f32[3072,16]{0,1:T(8,128)}, f32[16,2048]{1,0:T(8,128)}, f32[3072,16]{0,1:T(8,128)}, f32[16,1024]{1,0:T(8,128)}), (f32[3072,16]{0,1:T(8,128)}, f32[16,2048]{1,0:T(8,128)}, f32[3072,16]{0,1:T(8,128)}, ...) | async-done | bytes 589840 | tf_op jit(solution)/shard_map/psum | solution.py:169
  401.2 1.6 broadcast_multiply_fusion.2
  402.8 1.5 broadcast_multiply_fusion.3
  404.3 1.8 broadcast_multiply_fusion
  (165 shorter events, 32.5 us)
Async XLA Ops:
  7.2 79.7 %copy-start = (bf16[3072,16]{0,1:T(8,128)(2,1)S(1)}, bf16[3072,16]{0,1:T(8,128)(2,1)}, u32[]{:S(2)}) copy-start(bf16[3072,16]{0,1:T(8,128)(2,1)} %param.21) | copy-start | bytes 294916
  7.2 118.5 %copy-start.2 = (bf16[192,1024]{1,0:T(8,128)(2,1)S(1)}, bf16[192,1024]{1,0:T(8,128)(2,1)}, u32[]{:S(2)}) copy-start(bf16[192,1024]{1,0:T(8,128)(2,1)} %param.18) | copy-start | bytes 1179652
  7.2 126.2 %all-gather.3.cloned.1.call-start = ((), (), s32[]{:S(2)}) async-start(), calls=%async_computation | async-start | bytes 6684672 | tf_op jit(solution)/shard_map/all_gather | solution.py:100
  7.9 197.1 %all-gather.5.cloned.1.call-start = ((), (), s32[]{:S(2)}) async-start(), calls=%async_computation.1 | async-start | bytes 13369344 | tf_op jit(solution)/shard_map/all_gather | solution.py:98
  8.7 392.5 %all-reduce.3.cloned.1.call-start = ((), (), s32[]{:S(2)}) async-start(), calls=%async_computation.2 | async-start | bytes 1179648 | tf_op jit(solution)/shard_map/psum | solution.py:169
  8.7 11.2 %collective-permute-start.4 = (bf16[192,1024]{1,0:T(8,128)(2,1)}, bf16[192,1024]{1,0:T(8,128)(2,1)S(1)}, u32[]{:S(2)}, u32[]{:S(2)}) collective-permute-start(bf16[192,1024]{1,0:T(8,128)(2,1)} %param.18), channel_id=1, source_target_pairs={{0,1},{1,2},{2,3},{3,4},{4,5},{5,6},{6,7},{7,8},{8,9},{9,10},{10,1... | collective-permute-start | bytes 1179656 | tf_op jit(solution)/shard_map/ppermute | solution.py:20
  19.9 16.0 %collective-permute-start.5 = (bf16[192,1024]{1,0:T(8,128)(2,1)S(1)}, bf16[192,1024]{1,0:T(8,128)(2,1)S(1)}, u32[]{:S(2)}, u32[]{:S(2)}) collective-permute-start(bf16[192,1024]{1,0:T(8,128)(2,1)S(1)} %collective-permute-done.4), channel_id=1, source_target_pairs={{0,1},{1,2},{2,3},{3,4},{4,5},{5,6},{6,7},{7,8},{8,9},{9,10},{10,1... | collective-permute-start | bytes 1179656 | tf_op jit(solution)/shard_map/ppermute | solution.py:20
  19.9 16.0 %collective-permute-start.12 = (bf16[192,1024]{1,0:T(8,128)(2,1)}, bf16[192,1024]{1,0:T(8,128)(2,1)S(1)}, u32[]{:S(2)}, u32[]{:S(2)}) collective-permute-start(bf16[192,1024]{1,0:T(8,128)(2,1)} %param.18), channel_id=1, source_target_pairs={{0,15},{1,0},{2,1},{3,2},{4,3},{5,4},{6,5},{7,6},{8,7},{9,8},{10,9... | collective-permute-start | bytes 1179656 | tf_op jit(solution)/shard_map/ppermute | solution.py:22
  35.9 11.5 %collective-permute-start.6 = (bf16[192,1024]{1,0:T(8,128)(2,1)S(1)}, bf16[192,1024]{1,0:T(8,128)(2,1)S(1)}, u32[]{:S(2)}, u32[]{:S(2)}) collective-permute-start(bf16[192,1024]{1,0:T(8,128)(2,1)S(1)} %collective-permute-done.5), channel_id=1, source_target_pairs={{0,1},{1,2},{2,3},{3,4},{4,5},{5,6},{6,7},{7,8},{8,9},{9,10},{10,1... | collective-permute-start | bytes 1179656 | tf_op jit(solution)/shard_map/ppermute | solution.py:20
  35.9 11.5 %collective-permute-start.13 = (bf16[192,1024]{1,0:T(8,128)(2,1)S(1)}, bf16[192,1024]{1,0:T(8,128)(2,1)S(1)}, u32[]{:S(2)}, u32[]{:S(2)}) collective-permute-start(bf16[192,1024]{1,0:T(8,128)(2,1)S(1)} %collective-permute-done.12), channel_id=1, source_target_pairs={{0,15},{1,0},{2,1},{3,2},{4,3},{5,4},{6,5},{7,6},{8,7},{9,8},{10,9... | collective-permute-start | bytes 1179656 | tf_op jit(solution)/shard_map/ppermute | solution.py:22
  47.4 18.4 %copy-start.3 = (bf16[192,1024]{1,0:T(8,128)(2,1)}, bf16[192,1024]{1,0:T(8,128)(2,1)S(1)}, u32[]{:S(2)}) copy-start(bf16[192,1024]{1,0:T(8,128)(2,1)S(1)} %collective-permute-done.6) | copy-start | bytes 1179652
  47.4 18.3 %collective-permute-start.7 = (bf16[192,1024]{1,0:T(8,128)(2,1)S(1)}, bf16[192,1024]{1,0:T(8,128)(2,1)S(1)}, u32[]{:S(2)}, u32[]{:S(2)}) collective-permute-start(bf16[192,1024]{1,0:T(8,128)(2,1)S(1)} %collective-permute-done.6), channel_id=1, source_target_pairs={{0,1},{1,2},{2,3},{3,4},{4,5},{5,6},{6,7},{7,8},{8,9},{9,10},{10,1... | collective-permute-start | bytes 1179656 | tf_op jit(solution)/shard_map/ppermute | solution.py:20
  47.4 18.3 %collective-permute-start.14 = (bf16[192,1024]{1,0:T(8,128)(2,1)S(1)}, bf16[192,1024]{1,0:T(8,128)(2,1)S(1)}, u32[]{:S(2)}, u32[]{:S(2)}) collective-permute-start(bf16[192,1024]{1,0:T(8,128)(2,1)S(1)} %collective-permute-done.13), channel_id=1, source_target_pairs={{0,15},{1,0},{2,1},{3,2},{4,3},{5,4},{6,5},{7,6},{8,7},{9,8},{10,9... | collective-permute-start | bytes 1179656 | tf_op jit(solution)/shard_map/ppermute | solution.py:22
  65.7 4.5 %copy-start.9 = (bf16[192,1024]{1,0:T(8,128)(2,1)}, bf16[192,1024]{1,0:T(8,128)(2,1)S(1)}, u32[]{:S(2)}) copy-start(bf16[192,1024]{1,0:T(8,128)(2,1)S(1)} %collective-permute-done.7) | copy-start | bytes 1179652
  65.7 10.3 %collective-permute-start.8 = (bf16[192,1024]{1,0:T(8,128)(2,1)S(1)}, bf16[192,1024]{1,0:T(8,128)(2,1)S(1)}, u32[]{:S(2)}, u32[]{:S(2)}) collective-permute-start(bf16[192,1024]{1,0:T(8,128)(2,1)S(1)} %collective-permute-done.7), channel_id=1, source_target_pairs={{0,1},{1,2},{2,3},{3,4},{4,5},{5,6},{6,7},{7,8},{8,9},{9,10},{10,1... | collective-permute-start | bytes 1179656 | tf_op jit(solution)/shard_map/ppermute | solution.py:20
  65.8 33.4 %copy-start.5 = (bf16[192,1024]{1,0:T(8,128)(2,1)}, bf16[192,1024]{1,0:T(8,128)(2,1)S(1)}, u32[]{:S(2)}) copy-start(bf16[192,1024]{1,0:T(8,128)(2,1)S(1)} %collective-permute-done.14) | copy-start | bytes 1179652
  65.8 16.8 %collective-permute-start.15 = (bf16[192,1024]{1,0:T(8,128)(2,1)S(1)}, bf16[192,1024]{1,0:T(8,128)(2,1)S(1)}, u32[]{:S(2)}, u32[]{:S(2)}) collective-permute-start(bf16[192,1024]{1,0:T(8,128)(2,1)S(1)} %collective-permute-done.14), channel_id=1, source_target_pairs={{0,15},{1,0},{2,1},{3,2},{4,3},{5,4},{6,5},{7,6},{8,7},{9,8},{10,9... | collective-permute-start | bytes 1179656 | tf_op jit(solution)/shard_map/ppermute | solution.py:22
  76.1 24.2 %copy-start.11 = (bf16[192,1024]{1,0:T(8,128)(2,1)}, bf16[192,1024]{1,0:T(8,128)(2,1)S(1)}, u32[]{:S(2)}) copy-start(bf16[192,1024]{1,0:T(8,128)(2,1)S(1)} %collective-permute-done.8) | copy-start | bytes 1179652
  76.1 10.8 %collective-permute-start.9 = (bf16[192,1024]{1,0:T(8,128)(2,1)S(1)}, bf16[192,1024]{1,0:T(8,128)(2,1)S(1)}, u32[]{:S(2)}, u32[]{:S(2)}) collective-permute-start(bf16[192,1024]{1,0:T(8,128)(2,1)S(1)} %collective-permute-done.8), channel_id=1, source_target_pairs={{0,1},{1,2},{2,3},{3,4},{4,5},{5,6},{6,7},{7,8},{8,9},{9,10},{10,1... | collective-permute-start | bytes 1179656 | tf_op jit(solution)/shard_map/ppermute | solution.py:20
  76.8 65.0 %copy-start.16 = (bf16[128]{0:T(256)(128)(2,1)}, bf16[128]{0:T(256)(128)(2,1)S(1)}, u32[]{:S(2)}) copy-start(bf16[128]{0:T(256)(128)(2,1)S(1)} %convert_bitcast_fusion) | copy-start | bytes 772
  76.8 61.1 %collective-permute-start.2 = (bf16[128]{0:T(256)(128)(2,1)S(1)}, bf16[128]{0:T(256)(128)(2,1)S(1)}, u32[]{:S(2)}, u32[]{:S(2)}) collective-permute-start(bf16[128]{0:T(256)(128)(2,1)S(1)} %convert_bitcast_fusion), channel_id=1, source_target_pairs={} | collective-permute-start | bytes 776 | tf_op jit(solution)/shard_map/ppermute | solution.py:30
  77.5 64.4 %collective-permute-start.3 = (bf16[128]{0:T(256)(128)(2,1)S(1)}, bf16[128]{0:T(256)(128)(2,1)S(1)}, u32[]{:S(2)}, u32[]{:S(2)}) collective-permute-start(bf16[128]{0:T(256)(128)(2,1)S(1)} %convert_bitcast_fusion), channel_id=1, source_target_pairs={{0,16},{1,17},{2,18},{3,19},{4,20},{5,21},{6,22},{7,23},{8,24},{9,... | collective-permute-start | bytes 776 | tf_op jit(solution)/shard_map/ppermute | solution.py:30
  82.6 16.6 %copy-start.7 = (bf16[192,1024]{1,0:T(8,128)(2,1)}, bf16[192,1024]{1,0:T(8,128)(2,1)S(1)}, u32[]{:S(2)}) copy-start(bf16[192,1024]{1,0:T(8,128)(2,1)S(1)} %collective-permute-done.15) | copy-start | bytes 1179652
  82.6 11.8 %collective-permute-start.16 = (bf16[192,1024]{1,0:T(8,128)(2,1)S(1)}, bf16[192,1024]{1,0:T(8,128)(2,1)}, u32[]{:S(2)}, u32[]{:S(2)}) collective-permute-start(bf16[192,1024]{1,0:T(8,128)(2,1)S(1)} %collective-permute-done.15), channel_id=1, source_target_pairs={{0,15},{1,0},{2,1},{3,2},{4,3},{5,4},{6,5},{7,6},{8,7},{9,8},{10,9... | collective-permute-start | bytes 1179656 | tf_op jit(solution)/shard_map/ppermute | solution.py:22
  86.8 13.4 %copy-start.13 = (bf16[192,1024]{1,0:T(8,128)(2,1)}, bf16[192,1024]{1,0:T(8,128)(2,1)S(1)}, u32[]{:S(2)}) copy-start(bf16[192,1024]{1,0:T(8,128)(2,1)S(1)} %collective-permute-done.9) | copy-start | bytes 1179652
  86.8 12.4 %collective-permute-start.10 = (bf16[192,1024]{1,0:T(8,128)(2,1)S(1)}, bf16[192,1024]{1,0:T(8,128)(2,1)}, u32[]{:S(2)}, u32[]{:S(2)}) collective-permute-start(bf16[192,1024]{1,0:T(8,128)(2,1)S(1)} %collective-permute-done.9), channel_id=1, source_target_pairs={{0,1},{1,2},{2,3},{3,4},{4,5},{5,6},{6,7},{7,8},{8,9},{9,10},{10,1... | collective-permute-start | bytes 1179656 | tf_op jit(solution)/shard_map/ppermute | solution.py:20
  86.9 118.2 %copy-start.22 = (f32[128]{0:T(128)}, f32[128]{0:T(128)S(1)}, u32[]{:S(2)}) copy-start(f32[128]{0:T(128)S(1)} %add_rsqrt_fusion) | copy-start | bytes 1540
  88.5 38.5 %copy-start.18 = (bf16[128,16]{0,1:T(8,128)(2,1)}, bf16[128,16]{0,1:T(8,128)(2,1)S(1)}, u32[]{:S(2)}) copy-start(bf16[128,16]{0,1:T(8,128)(2,1)S(1)} %convolution_convert_fusion.2) | copy-start | bytes 12292
  94.4 10.4 %collective-permute-start.17 = (bf16[192,1024]{1,0:T(8,128)(2,1)}, bf16[192,1024]{1,0:T(8,128)(2,1)}, u32[]{:S(2)}, u32[]{:S(2)}) collective-permute-start(bf16[192,1024]{1,0:T(8,128)(2,1)} %collective-permute-done.16), channel_id=1, source_target_pairs={{0,15},{1,0},{2,1},{3,2},{4,3},{5,4},{6,5},{7,6},{8,7},{9,8},{10,9... | collective-permute-start | bytes 1179656 | tf_op jit(solution)/shard_map/ppermute | solution.py:22
  99.2 10.3 %collective-permute-start.11 = (bf16[192,1024]{1,0:T(8,128)(2,1)}, bf16[192,1024]{1,0:T(8,128)(2,1)}, u32[]{:S(2)}, u32[]{:S(2)}) collective-permute-start(bf16[192,1024]{1,0:T(8,128)(2,1)} %collective-permute-done.10), channel_id=1, source_target_pairs={{0,1},{1,2},{2,3},{3,4},{4,5},{5,6},{6,7},{7,8},{8,9},{9,10},{10,1... | collective-permute-start | bytes 1179656 | tf_op jit(solution)/shard_map/ppermute | solution.py:20
  100.3 25.2 %copy-start.14 = (bf16[192,1024]{1,0:T(8,128)(2,1)S(1)}, bf16[192,1024]{1,0:T(8,128)(2,1)}, u32[]{:S(2)}) copy-start(bf16[192,1024]{1,0:T(8,128)(2,1)} %copy-done.13) | copy-start | bytes 1179652
  100.3 25.2 %copy-start.12 = (bf16[192,1024]{1,0:T(8,128)(2,1)S(1)}, bf16[192,1024]{1,0:T(8,128)(2,1)}, u32[]{:S(2)}) copy-start(bf16[192,1024]{1,0:T(8,128)(2,1)} %copy-done.11) | copy-start | bytes 1179652
  100.3 25.3 %copy-start.10 = (bf16[192,1024]{1,0:T(8,128)(2,1)S(1)}, bf16[192,1024]{1,0:T(8,128)(2,1)}, u32[]{:S(2)}) copy-start(bf16[192,1024]{1,0:T(8,128)(2,1)} %copy-done.9) | copy-start | bytes 1179652
  100.3 25.3 %copy-start.4 = (bf16[192,1024]{1,0:T(8,128)(2,1)S(1)}, bf16[192,1024]{1,0:T(8,128)(2,1)}, u32[]{:S(2)}) copy-start(bf16[192,1024]{1,0:T(8,128)(2,1)} %copy-done.3) | copy-start | bytes 1179652
  100.3 25.5 %copy-start.6 = (bf16[192,1024]{1,0:T(8,128)(2,1)S(1)}, bf16[192,1024]{1,0:T(8,128)(2,1)}, u32[]{:S(2)}) copy-start(bf16[192,1024]{1,0:T(8,128)(2,1)} %copy-done.5) | copy-start | bytes 1179652
  100.3 25.6 %copy-start.8 = (bf16[192,1024]{1,0:T(8,128)(2,1)S(1)}, bf16[192,1024]{1,0:T(8,128)(2,1)}, u32[]{:S(2)}) copy-start(bf16[192,1024]{1,0:T(8,128)(2,1)} %copy-done.7) | copy-start | bytes 1179652
  102.5 109.0 %copy-start.19 = (bf16[128,16]{0,1:T(8,128)(2,1)}, bf16[128,16]{0,1:T(8,128)(2,1)S(1)}, u32[]{:S(2)}) copy-start(bf16[128,16]{0,1:T(8,128)(2,1)S(1)} %convolution_convert_fusion.3) | copy-start | bytes 12292
  102.5 25.5 %copy-start.1 = (bf16[1,128,3072]{2,1,0:T(8,128)(2,1)S(1)}, bf16[1,128,3072]{2,1,0:T(8,128)(2,1)}, u32[]{:S(2)}) copy-start(bf16[1,128,3072]{2,1,0:T(8,128)(2,1)} %param.13) | copy-start | bytes 2359300
  104.8 18.6 %collective-permute-start.18 = (bf16[192,1024]{1,0:T(8,128)(2,1)}, bf16[192,1024]{1,0:T(8,128)(2,1)S(1)}, u32[]{:S(2)}, u32[]{:S(2)}) collective-permute-start(bf16[192,1024]{1,0:T(8,128)(2,1)} %collective-permute-done.17), channel_id=1, source_target_pairs={{0,15},{1,0},{2,1},{3,2},{4,3},{5,4},{6,5},{7,6},{8,7},{9,8},{10,9... | collective-permute-start | bytes 1179656 | tf_op jit(solution)/shard_map/ppermute | solution.py:22
  130.1 11.8 %collective-permute-start.19 = (bf16[128,1024]{1,0:T(8,128)(2,1)S(1)}, bf16[128,1024]{1,0:T(8,128)(2,1)S(1)}, u32[]{:S(2)}, u32[]{:S(2)}) collective-permute-start(bf16[128,1024]{1,0:T(8,128)(2,1)S(1)} %fusion.65), channel_id=1, source_target_pairs={} | collective-permute-start | bytes 786440 | tf_op jit(solution)/shard_map/ppermute | solution.py:30
  130.8 11.2 %collective-permute-start.20 = (bf16[128,1024]{1,0:T(8,128)(2,1)S(1)}, bf16[128,1024]{1,0:T(8,128)(2,1)S(1)}, u32[]{:S(2)}, u32[]{:S(2)}) collective-permute-start(bf16[128,1024]{1,0:T(8,128)(2,1)S(1)} %fusion.65), channel_id=1, source_target_pairs={{0,16},{1,17},{2,18},{3,19},{4,20},{5,21},{6,22},{7,23},{8,24},{9,... | collective-permute-start | bytes 786440 | tf_op jit(solution)/shard_map/ppermute | solution.py:30
  137.3 4.8 %collective-permute-start = (bf16[128,1024]{1,0:T(8,128)(2,1)S(1)}, bf16[128,1024]{1,0:T(8,128)(2,1)S(1)}, u32[]{:S(2)}, u32[]{:S(2)}) collective-permute-start(bf16[128,1024]{1,0:T(8,128)(2,1)S(1)} %convolution_convert_fusion), channel_id=1, source_target_pairs={} | collective-permute-start | bytes 786440 | tf_op jit(solution)/shard_map/ppermute | solution.py:30
  138.0 5.2 %collective-permute-start.1 = (bf16[128,1024]{1,0:T(8,128)(2,1)S(1)}, bf16[128,1024]{1,0:T(8,128)(2,1)}, u32[]{:S(2)}, u32[]{:S(2)}) collective-permute-start(bf16[128,1024]{1,0:T(8,128)(2,1)S(1)} %convolution_convert_fusion), channel_id=1, source_target_pairs={{0,16},{1,17},{2,18},{3,19},{4,20},{5,21},{6,22},{7,23},{8,24},{9,... | collective-permute-start | bytes 786440 | tf_op jit(solution)/shard_map/ppermute | solution.py:30
  145.1 68.8 %copy-start.17 = (bf16[128]{0:T(256)(128)(2,1)S(1)}, bf16[128]{0:T(256)(128)(2,1)}, u32[]{:S(2)}) copy-start(bf16[128]{0:T(256)(128)(2,1)} %copy-done.16) | copy-start | bytes 772
  145.1 68.8 %copy-start.20 = (s32[128]{0:T(128)S(1)}, s32[128]{0:T(128)}, u32[]{:S(2)}) copy-start(s32[128]{0:T(128)} %iota_add_fusion) | copy-start | bytes 1540
  145.2 68.8 %copy-start.21 = (pred[384]{0:T(512)(128)(4,1)S(1)}, pred[384]{0:T(512)(128)(4,1)}, u32[]{:S(2)}) copy-start(pred[384]{0:T(512)(128)(4,1)} %fusion.71) | copy-start | bytes 1156
  214.0 55.8 %copy-start.15 = (bf16[16,1024]{1,0:T(8,128)(2,1)S(1)}, bf16[16,1024]{1,0:T(8,128)(2,1)}, u32[]{:S(2)}) copy-start(bf16[16,1024]{1,0:T(8,128)(2,1)} %param.22) | copy-start | bytes 98308
  253.8 16.0 %collective-permute-start.21 = (f32[128,1024]{0,1:T(8,128)S(1)}, f32[128,1024]{0,1:T(8,128)S(1)}, u32[]{:S(2)}, u32[]{:S(2)}) collective-permute-start(f32[128,1024]{0,1:T(8,128)S(1)} %bitcast.192), channel_id=1, source_target_pairs={{16,0},{17,1},{18,2},{19,3},{20,4},{21,5},{22,6},{23,7},{24,8},{25... | collective-permute-start | bytes 1572872 | tf_op jit(solution)/shard_map/ppermute | solution.py:30
  255.1 14.7 %collective-permute-start.22 = (f32[128,1024]{0,1:T(8,128)S(1)}, f32[128,1024]{0,1:T(8,128)S(1)}, u32[]{:S(2)}, u32[]{:S(2)}) collective-permute-start(f32[128,1024]{0,1:T(8,128)S(1)} %bitcast.191), channel_id=1, source_target_pairs={} | collective-permute-start | bytes 1572872 | tf_op jit(solution)/shard_map/ppermute | solution.py:30
Sparse Core Ops, SparseCore 0:
  10.3 87.6 all-gather.2
  100.2 104.7 all-gather.4
  274.1 127.0 all-reduce.2
